TPU v7x, 256 devices: a whole 4x4x8 slice. The times are simulated.
256 devices in a mesh: req: 64 (over y, z, core), tp: 4 (over x).
Axes of the slice: x: 4, y: 4, z: 8, core: 2. Of those that a mesh axis runs over, the one named last changes fastest.
Arguments:
- patches: bfloat16 [16384, 1280], P('req'), may hold values from -6 to 6
- half_grid: int32 [64, 2], P('req'), may hold values from 6 to 8
- text_embed: bfloat16 [12288, 1280], P('req'), may hold values from -6 to 6
- dest_dev: int32 [4096], P('req'), may hold values from 0 to 63, as said below
- dest_pos: int32 [4096], P('req'), may hold values from 0 to 191, as said below
- text_len: int32 [64], P('req'), may hold values from 1 to 128, as said below
- enc_qkv: bfloat16 [1280, 3840], P('req', 'tp')
- enc_out_t: bfloat16 [1280, 1280], P('req', 'tp'), may hold values from -0.15625 to 0.15625
- enc_up: bfloat16 [1280, 5120], P('req', 'tp'), may hold values from -0.15625 to 0.15625
- enc_down_t: bfloat16 [1280, 5120], P('req', 'tp'), may hold values from -0.078125 to 0.078125
- merge_t: bfloat16 [1280, 5120], P('req', 'tp'), may hold values from -0.078125 to 0.078125
- dec_qkv: bfloat16 [1280, 3840], P('req', 'tp')
- dec_out_t: bfloat16 [1280, 1280], P('req', 'tp'), may hold values from -0.15625 to 0.15625
- dec_up: bfloat16 [1280, 5120], P('req', 'tp'), may hold values from -0.15625 to 0.15625
- dec_down_t: bfloat16 [1280, 5120], P('req', 'tp'), may hold values from -0.078125 to 0.078125
Outputs:
- decoded: bfloat16 [12288, 1280], P('req')
Inputs may be any that keep to these rules, and one draw needn't show every extreme that they name: `dest_dev`: the slots of one device go in runs to destination devices; at most 2 slots of one device name one destination device, exactly 2 for some pairs; every device is named by exactly 64 slots in all. `dest_pos`: positions named for one destination device are distinct and below 64 plus its text_len. `text_len`: some request has exactly 128.
All inputs are finite; a program needn't handle non-finite values.
Results may differ from a plain program's by a relative error of at most 0.024.
Values may be sent and summed in bfloat16 or wider, within the bound.
A program may use at most 64 MiB of HBM per device.

v0:
```python
import jax
import jax.numpy as jnp
from jax import lax
from jax.sharding import PartitionSpec as P

HEAD_DIM = 80
GRID = 16


EPS = 1e-06


def for_sending(shard):

    def short(part):
        return part.astype(jnp.bfloat16) if part.dtype == jnp.float32 else part

    return jax.tree.map(short, shard)


def normalize(stream):
    values_f = stream.astype(jnp.float32)
    center = values_f - jnp.mean(values_f, axis=-1, keepdims=True)
    spread = jnp.mean(center * center, axis=-1, keepdims=True)
    return (center * lax.rsqrt(spread + EPS)).astype(jnp.bfloat16)


def fetch_weights(weights):
    return jax.tree.map(
        lambda part, own: part.astype(own.dtype),
        lax.all_gather(for_sending(weights), "req", axis=0, tiled=True),
        weights,
    )


def tensor_total(partial_value):
    return lax.psum(partial_value.astype(jnp.bfloat16), "tp").astype(jnp.float32)


def attention(normed, w_qkv, w_out_t, allowed, sample_count):
    total_rows = normed.shape[0]
    length = total_rows // sample_count
    projected = jnp.dot(normed, w_qkv, preferred_element_type=jnp.float32).astype(jnp.bfloat16)
    projected = projected.reshape(sample_count, length, -1, 3, HEAD_DIM)
    queries = projected[:, :, :, 0]
    key_part = projected[:, :, :, 1]
    value_part = projected[:, :, :, 2]
    scores = jnp.einsum(
        "bqhd,bkhd->bhqk", queries, key_part, preferred_element_type=jnp.float32
    ) * HEAD_DIM ** (-0.5)
    scores = jnp.where(allowed, scores, -1e30)
    highest = jnp.max(scores, axis=-1, keepdims=True)
    exponent = jnp.exp(scores - highest)
    weights_soft = (exponent / jnp.sum(exponent, axis=-1, keepdims=True)).astype(jnp.bfloat16)
    heads_out = jnp.einsum(
        "bhqk,bkhd->bqhd", weights_soft, value_part, preferred_element_type=jnp.float32
    )
    heads_out = heads_out.astype(jnp.bfloat16).reshape(total_rows, -1)
    return lax.dot_general(
        heads_out, w_out_t, (((1,), (1,)), ((), ())), preferred_element_type=jnp.float32
    )


def feed_forward(normed, w_up, w_down_t):
    hidden = jax.nn.gelu(
        jnp.dot(normed, w_up, preferred_element_type=jnp.float32), approximate=False
    )
    hidden = hidden.astype(jnp.bfloat16)
    return lax.dot_general(
        hidden, w_down_t, (((1,), (1,)), ((), ())), preferred_element_type=jnp.float32
    )


def transformer_layer(stream, weights, allowed, sample_count):
    w_qkv, w_out_t, w_up, w_down_t = weights
    attended = attention(normalize(stream), w_qkv, w_out_t, allowed, sample_count)
    middle = (stream.astype(jnp.float32) + tensor_total(attended)).astype(jnp.bfloat16)
    result_rows = middle.astype(jnp.float32) + tensor_total(
        feed_forward(normalize(middle), w_up, w_down_t)
    )
    result_rows = result_rows.astype(jnp.bfloat16)
    return result_rows


def on_device(
    patches,
    half_grid,
    text_embed,
    dest_dev,
    dest_pos,
    text_len,
    enc_qkv,
    enc_out_t,
    enc_up,
    enc_down_t,
    merge_t,
    dec_qkv,
    dec_out_t,
    dec_up,
    dec_down_t,
):
    image_count = half_grid.shape[0]
    model_width = patches.shape[1]
    per_image = GRID * GRID
    patch_index = jnp.arange(per_image, dtype=jnp.int32)
    key_valid = ((patch_index // GRID)[None, :] < 2 * half_grid[:, 0:1]) & (
        (patch_index % GRID)[None, :] < 2 * half_grid[:, 1:2]
    )
    enc_weights = fetch_weights((enc_qkv, enc_out_t, enc_up, enc_down_t))
    encoded = transformer_layer(patches, enc_weights, key_valid[:, None, None, :], image_count)
    merge_local, qkv_dec, out_dec, up_dec, down_dec = fetch_weights(
        (merge_t, dec_qkv, dec_out_t, dec_up, dec_down_t)
    )
    half_side = GRID // 2
    blocks = encoded.reshape(image_count, half_side, 2, half_side, 2, model_width).transpose(
        0, 1, 3, 2, 4, 5
    )
    blocks = blocks.reshape(image_count * half_side * half_side, 4 * model_width)
    span_width = merge_local.shape[1]
    feature_part = lax.dynamic_slice_in_dim(
        blocks, lax.axis_index("tp") * span_width, span_width, 1
    )
    merge_partial = lax.dot_general(
        feature_part, merge_local, (((1,), (1,)), ((), ())), preferred_element_type=jnp.float32
    )
    merged = tensor_total(merge_partial).astype(jnp.bfloat16)
    slot_count = merged.shape[0]
    senders = lax.axis_size("req")
    even_share = slot_count // senders
    capacity = even_share + max(even_share // 2, 1)
    cell_index = jnp.arange(half_side * half_side, dtype=jnp.int32)
    slot_valid = ((cell_index // half_side)[None, :] < half_grid[:, 0:1]) & (
        (cell_index % half_side)[None, :] < half_grid[:, 1:2]
    )
    slot_valid = slot_valid.reshape(slot_count)
    one_hot = (dest_dev[:, None] == jnp.arange(senders, dtype=jnp.int32)[None, :]).astype(jnp.int32)
    earlier = jnp.cumsum(one_hot, axis=0) - one_hot
    slot_rank = jnp.sum(earlier * one_hot, axis=1)
    outgoing = (
        jnp.zeros((senders, capacity, model_width), jnp.bfloat16)
        .at[dest_dev, slot_rank]
        .set(merged)
    )
    out_pos = (
        jnp.full((senders, capacity), -1, jnp.int32)
        .at[dest_dev, slot_rank]
        .set(jnp.where(slot_valid, dest_pos, -1))
    )
    incoming, in_pos = (
        lax.all_to_all(outgoing, "req", split_axis=0, concat_axis=0, tiled=True),
        lax.all_to_all(out_pos, "req", split_axis=0, concat_axis=0, tiled=True),
    )
    seq_len = text_embed.shape[0]
    target = jnp.where(in_pos >= 0, in_pos, seq_len).astype(jnp.int32).reshape(-1)
    dec_input = text_embed.at[target].set(incoming.reshape(-1, model_width), mode="drop")
    positions = jnp.arange(seq_len, dtype=jnp.int32)
    causal = (positions[:, None] >= positions[None, :])[None, None]
    decoded = transformer_layer(dec_input, (qkv_dec, out_dec, up_dec, down_dec), causal, 1)
    keep_mask = positions < slot_count + text_len[0]
    return jnp.where(keep_mask[:, None], decoded, jnp.zeros_like(decoded))


def solution(mesh):
    return jax.shard_map(
        on_device,
        mesh=mesh,
        in_specs=(
            P("req", None),
            P("req", None),
            P("req", None),
            P("req"),
            P("req"),
            P("req"),
            P("req", "tp"),
            P("req", "tp"),
            P("req", "tp"),
            P("req", "tp"),
            P("req", "tp"),
            P("req", "tp"),
            P("req", "tp"),
            P("req", "tp"),
            P("req", "tp"),
        ),
        out_specs=P("req", None),
        check_vma=False,
    )
```

profile of v0, /device:TPU:8, one launch (start us, length us, event | category | flops | bytes accessed | tf_op | source)
XLA Modules:
  0.0 852.3 jit_solution(17187715245024345156)
XLA Ops:
  6.5 0.7 all-gather.17.cloned.1.call-update
  7.3 1.4 fusion.214
  10.0 53.3 %all-gather.1 = bf16[64,20,320]{2,1,0:T(8,128)(2,1)S(1)} all-gather(bf16[1,20,320]{2,1,0:T(8,128)(2,1)} %bitcast.120), channel_id=1, replica_groups=mesh['req'=64,'tp'=4] {'req'}, dimensions={0}, use_global_device_ids=true | all-gather | bytes 832000 | tf_op jit(solution)/shard_map/all_gather | solution.py:31
  63.3 0.4 reshape.279
  63.7 0.6 copy-done.1
  64.6 0.3 fusion.12
  64.9 25.2 %all-gather.17.cloned.1.call-done = bf16[64,20,960]{2,1,0:T(8,128)(2,1)} async-done(((bf16[1,20,960]{2,1,0:T(8,128)(2,1)}), bf16[64,20,960]{2,1,0:T(8,128)(2,1)}) %all-gather.17.cloned.1.call-update) | async-done | bytes 2457616 | tf_op jit(solution)/shard_map/all_gather | solution.py:31
  90.1 5.5 reshape.277
  95.6 2.9 convolution_convert_fusion.5
  98.5 0.3 fusion.9
  98.9 0.5 fusion.215
  99.4 0.4 convolution_convert_fusion.8
  99.8 1.4 convolution_convert_fusion
  101.3 0.7 all-gather.19.cloned.1.call-update
  102.1 0.5 all-gather.21.cloned.1.call-update
  102.6 0.5 all-gather.23.cloned.1.call-update
  103.2 45.6 %all-reduce.6.cloned.1.call-done = bf16[256,1280]{1,0:T(8,128)(2,1)} async-done(((bf16[256,1280]{1,0:T(8,128)(2,1)}), bf16[256,1280]{1,0:T(8,128)(2,1)}) %all-reduce.6.cloned.1.call-update) | async-done | bytes 655376 | tf_op jit(solution)/shard_map/psum | solution.py:37
  148.8 1.4 convert_reduce_fusion
  150.5 79.6 %all-gather.19.cloned.1.call-done = bf16[64,20,1280]{2,1,0:T(8,128)(2,1)} async-done(((bf16[1,20,1280]{2,1,0:T(8,128)(2,1)}), bf16[64,20,1280]{2,1,0:T(8,128)(2,1)}) %all-gather.19.cloned.1.call-update) | async-done | bytes 3276816 | tf_op jit(solution)/shard_map/all_gather | solution.py:31
  230.1 6.1 reshape.281
  236.2 72.5 %all-gather.21.cloned.1.call-done = bf16[64,20,1280]{2,1,0:T(8,128)(2,1)} async-done(((bf16[1,20,1280]{2,1,0:T(8,128)(2,1)}), bf16[64,20,1280]{2,1,0:T(8,128)(2,1)}) %all-gather.21.cloned.1.call-update) | async-done | bytes 3276816 | tf_op jit(solution)/shard_map/all_gather | solution.py:31
  308.7 6.1 reshape.283
  314.8 8.2 convolution_convert_fusion.1
  323.3 64.0 %all-gather.23.cloned.1.call-done = bf16[64,20,1280]{2,1,0:T(8,128)(2,1)} async-done(((bf16[1,20,1280]{2,1,0:T(8,128)(2,1)}), bf16[64,20,1280]{2,1,0:T(8,128)(2,1)}) %all-gather.23.cloned.1.call-update) | async-done | bytes 3276816 | tf_op jit(solution)/shard_map/all_gather | solution.py:31
  387.3 4.6 reshape.285
  391.9 44.6 %all-reduce.8.cloned.1.call-done = bf16[256,1280]{1,0:T(8,128)(2,1)} async-done(((bf16[256,1280]{1,0:T(8,128)(2,1)}), bf16[256,1280]{1,0:T(8,128)(2,1)}) %all-reduce.8.cloned.1.call-update) | async-done | bytes 655376 | tf_op jit(solution)/shard_map/psum | solution.py:37
  436.5 2.3 fusion.15
  438.8 2.6 reshape.248
  441.4 2.4 copy.56
  443.8 2.9 reshape.249
  446.7 2.7 convolution_convert_fusion.4
  449.5 0.7 all-gather.25.cloned.1.call-update
  450.3 0.7 all-gather.27.cloned.1.call-update
  451.0 0.5 all-gather.29.cloned.1.call-update
  451.9 1.3 and_select_fusion.2
  453.2 3.5 scatter_fusion
  456.7 0.7 copy.36
  457.4 10.6 %all-to-all-start = ((s32[64,1,2]{2,1,0:T(1,128)}), s32[64,1,2]{2,1,0:T(1,128)S(1)}, u32[]{:S(2)}, u32[]{:S(2)}) async-start(s32[64,1,2]{2,1,0:T(1,128)} %copy.36), calls=%async_computation | async-start | bytes 65536 | tf_op jit(solution)/shard_map/all_to_all | solution.py:151
  468.0 28.8 %all-reduce.10.cloned.1.call-done = bf16[64,1280]{1,0:T(8,128)(2,1)} async-done(((bf16[64,1280]{1,0:T(8,128)(2,1)}), bf16[64,1280]{1,0:T(8,128)(2,1)}) %all-reduce.10.cloned.1.call-update) | async-done | bytes 163856 | tf_op jit(solution)/shard_map/psum | solution.py:37
  496.8 0.9 broadcast_in_dim.47
  497.7 10.0 %scatter_fusion.1 = bf16[64,2,1280]{2,1,0:T(2,128)(2,1)} fusion(bf16[64,2,1280]{2,1,0:T(2,128)(2,1)} %broadcast_in_dim.47, s32[64]{0:T(128)S(1)} %fusion.146, bf16[64,1280]{1,0:T(8,128)(2,1)} %all-reduce.10.cloned.1.call-done), kind=kCustom, calls=%fused_computation.1 | custom fusion | bytes 492032 | tf_op jit(solution)/shard_map/scatter | solution.py:142
  507.7 10.6 %all-to-all-start.1 = ((bf16[64,2,1280]{2,1,0:T(2,128)(2,1)}), bf16[64,2,1280]{2,1,0:T(2,128)(2,1)S(1)}, u32[]{:S(2)}, u32[]{:S(2)}) async-start(bf16[64,2,1280]{2,1,0:T(2,128)(2,1)} %scatter_fusion.1), calls=%async_computation.1 | async-start | bytes 655360 | tf_op jit(solution)/shard_map/all_to_all | solution.py:150
  518.4 54.4 %all-gather.6 = bf16[64,20,320]{2,1,0:T(8,128)(2,1)S(1)} all-gather(bf16[1,20,320]{2,1,0:T(8,128)(2,1)S(1)} %bitcast.121), channel_id=1, replica_groups=mesh['req'=64,'tp'=4] {'req'}, dimensions={0}, use_global_device_ids=true | all-gather | bytes 832000 | tf_op jit(solution)/shard_map/all_gather | solution.py:31
  572.8 0.4 reshape.289
  573.3 0.5 broadcast.367
  573.8 0.6 reduce.11
  574.5 4.0 all-gather.25.cloned.1.call-done
  578.5 5.5 reshape.287
  584.2 0.9 copy-done
  585.1 1.6 scatter_fusion.2
  587.1 2.5 convolution_convert_fusion.6
  589.8 0.5 fusion.216
  590.3 0.3 fusion.27
  590.6 0.3 convolution_convert_fusion.7
  590.9 1.3 convolution_convert_fusion.3
  592.3 65.9 %all-gather.27.cloned.1.call-done = bf16[64,20,1280]{2,1,0:T(8,128)(2,1)} async-done(((bf16[1,20,1280]{2,1,0:T(8,128)(2,1)}), bf16[64,20,1280]{2,1,0:T(8,128)(2,1)}) %all-gather.27.cloned.1.call-update) | async-done | bytes 3276816 | tf_op jit(solution)/shard_map/all_gather | solution.py:31
  658.2 6.1 reshape.291
  664.3 72.8 %all-gather.29.cloned.1.call-done = bf16[64,20,1280]{2,1,0:T(8,128)(2,1)} async-done(((bf16[1,20,1280]{2,1,0:T(8,128)(2,1)}), bf16[64,20,1280]{2,1,0:T(8,128)(2,1)}) %all-gather.29.cloned.1.call-update) | async-done | bytes 3276816 | tf_op jit(solution)/shard_map/all_gather | solution.py:31
  737.1 6.1 reshape.293
  743.2 42.6 %all-reduce.12.cloned.1.call-done = bf16[192,1280]{1,0:T(8,128)(2,1)} async-done(((bf16[192,1280]{1,0:T(8,128)(2,1)}), bf16[192,1280]{1,0:T(8,128)(2,1)}) %all-reduce.12.cloned.1.call-update) | async-done | bytes 491536 | tf_op jit(solution)/shard_map/psum | solution.py:37
  785.8 1.3 convert_reduce_fusion.2
  787.4 7.4 convolution_convert_fusion.2
  795.5 48.0 %all-reduce.14.cloned.1.call-done = bf16[192,1280]{1,0:T(8,128)(2,1)} async-done(((bf16[192,1280]{1,0:T(8,128)(2,1)}), bf16[192,1280]{1,0:T(8,128)(2,1)}) %all-reduce.14.cloned.1.call-update) | async-done | bytes 491536 | tf_op jit(solution)/shard_map/psum | solution.py:37
  843.5 2.0 fusion.93
  (54 shorter events, 2.8 us)
Async XLA Ops:
  6.5 83.6 %all-gather.17.cloned.1.call-start = ((), (), s32[]{:S(2)}) async-start(), calls=%async_computation.7 | async-start | bytes 3194880 | tf_op jit(solution)/shard_map/all_gather | solution.py:31
  7.3 141.5 %all-reduce.6.cloned.1.call-start = ((), (), s32[]{:S(2)}) async-start(), calls=%async_computation.2 | async-start | bytes 1310720 | tf_op jit(solution)/shard_map/psum | solution.py:37
  63.3 1.1 copy-start.1
  101.3 128.8 %all-gather.19.cloned.1.call-start = ((), (), s32[]{:S(2)}) async-start(), calls=%async_computation.8 | async-start | bytes 3993600 | tf_op jit(solution)/shard_map/all_gather | solution.py:31
  102.0 206.7 %all-gather.21.cloned.1.call-start = ((), (), s32[]{:S(2)}) async-start(), calls=%async_computation.9 | async-start | bytes 3993600 | tf_op jit(solution)/shard_map/all_gather | solution.py:31
  102.6 284.7 %all-gather.23.cloned.1.call-start = ((), (), s32[]{:S(2)}) async-start(), calls=%async_computation.10 | async-start | bytes 3993600 | tf_op jit(solution)/shard_map/all_gather | solution.py:31
  103.2 333.4 %all-reduce.8.cloned.1.call-start = ((), (), s32[]{:S(2)}) async-start(), calls=%async_computation.3 | async-start | bytes 1310720 | tf_op jit(solution)/shard_map/psum | solution.py:37
  150.1 164.6 %copy-start.2 = (bf16[256,1280]{1,0:T(8,128)(2,1)}, bf16[256,1280]{1,0:T(8,128)(2,1)S(1)}, u32[]{:S(2)}) copy-start(bf16[256,1280]{1,0:T(8,128)(2,1)S(1)} %get-tuple-element.8) | copy-start | bytes 1966084
  323.0 173.8 %all-reduce.10.cloned.1.call-start = ((), (), s32[]{:S(2)}) async-start(), calls=%async_computation.4 | async-start | bytes 327680 | tf_op jit(solution)/shard_map/psum | solution.py:37
  446.7 4.8 copy-start.4
  446.7 5.2 copy-start.5
  449.5 129.1 %all-gather.25.cloned.1.call-start = ((), (), s32[]{:S(2)}) async-start(), calls=%async_computation.11 | async-start | bytes 3194880 | tf_op jit(solution)/shard_map/all_gather | solution.py:31
  450.2 208.0 %all-gather.27.cloned.1.call-start = ((), (), s32[]{:S(2)}) async-start(), calls=%async_computation.12 | async-start | bytes 3993600 | tf_op jit(solution)/shard_map/all_gather | solution.py:31
  451.0 286.2 %all-gather.29.cloned.1.call-start = ((), (), s32[]{:S(2)}) async-start(), calls=%async_computation.13 | async-start | bytes 3993600 | tf_op jit(solution)/shard_map/all_gather | solution.py:31
  457.4 50.3 %all-to-all-start = ((s32[64,1,2]{2,1,0:T(1,128)}), s32[64,1,2]{2,1,0:T(1,128)S(1)}, u32[]{:S(2)}, u32[]{:S(2)}) async-start(s32[64,1,2]{2,1,0:T(1,128)} %copy.36), calls=%async_computation | async-start | bytes 65536 | tf_op jit(solution)/shard_map/all_to_all | solution.py:151
  497.7 20.6 %copy-start.3 = (bf16[20,320]{1,0:T(8,128)(2,1)S(1)}, bf16[20,320]{1,0:T(8,128)(2,1)}, u32[]{:S(2)}) copy-start(bf16[20,320]{1,0:T(8,128)(2,1)} %param.27) | copy-start | bytes 38404
  507.7 76.3 %all-to-all-start.1 = ((bf16[64,2,1280]{2,1,0:T(2,128)(2,1)}), bf16[64,2,1280]{2,1,0:T(2,128)(2,1)S(1)}, u32[]{:S(2)}, u32[]{:S(2)}) async-start(bf16[64,2,1280]{2,1,0:T(2,128)(2,1)} %scatter_fusion.1), calls=%async_computation.1 | async-start | bytes 655360 | tf_op jit(solution)/shard_map/all_to_all | solution.py:150
  518.3 267.5 %all-reduce.12.cloned.1.call-start = ((), (), s32[]{:S(2)}) async-start(), calls=%async_computation.5 | async-start | bytes 983040 | tf_op jit(solution)/shard_map/psum | solution.py:37
  584.0 1.0 copy-start
  592.3 251.2 %all-reduce.14.cloned.1.call-start = ((), (), s32[]{:S(2)}) async-start(), calls=%async_computation.6 | async-start | bytes 983040 | tf_op jit(solution)/shard_map/psum | solution.py:37
Sparse Core Ops, SparseCore 0:
  10.1 79.9 all-gather.16
  101.4 47.3 all-reduce.5
  151.5 78.5 all-gather.18
  232.6 76.0 all-gather.20
  311.2 76.0 all-gather.22
  389.5 47.0 all-reduce.7
  449.6 47.2 all-reduce.9
  500.0 78.5 all-gather.24
  581.6 76.5 all-gather.26
  661.1 76.0 all-gather.28
  739.6 46.1 all-reduce.11
  794.9 48.4 all-reduce.13
where the time goes:
time: 854 us; the launch traced here: 852 us
  waiting for transfers between devices  598 us (70%)
  blocking collectives  108 us (13%)
  local copies, waits for them, and re-layouts  69.4 us (8%)
  matrix products  28.9 us (3%)
  starting transfers between devices  21.7 us (3%)
  between operations  15.7 us (2%)
  other arithmetic  10.7 us (1%)
    all_gather x7, waiting for transfers between devices, fetch_weights(): lax.all_gather(for_sending(weights), 'req', axis=0, tiled=True)  384 us
    psum x5, waiting for transfers between devices, tensor_total(): lax.psum(partial_value.astype(jnp.bfloat16), 'tp').astype(jnp.float32)  210 us
    all_gather x2, blocking collectives, fetch_weights(): lax.all_gather(for_sending(weights), 'req', axis=0, tiled=True)  108 us
    unnamed x21, local copies, waits for them, and re-layouts  42.5 us
  transfers between devices with their start and end apart: 14, of which 12 were waited for; matrix products, arithmetic and copies ran while one was open for 8% of the time, Pallas kernels for 0%

commit v1 on v0

--- a/solution.py
+++ b/solution.py
@@ -1,21 +1,326 @@
+import functools
+
 import jax
 import jax.numpy as jnp
 from jax import lax
+from jax.experimental import pallas as pl
+from jax.experimental.pallas import tpu as pltpu
 from jax.sharding import PartitionSpec as P
+
+MESH = pl.DeviceIdType.MESH
+NY, NZ, NX = 4, 8, 4
+GROUPS = 7
+D = 1280
+HALF = 640
+SHARD = 20
+EVENTS = 11
+CHIP_EVENTS = 8
+
+
+class Place:
+    def __init__(self):
+        req = lax.axis_index("req")
+        self.x = lax.axis_index("tp")
+        self.c = lax.rem(req, 2)
+        self.z = lax.rem(req // 2, NZ)
+        self.y = req // (2 * NZ)
+
+    def yy(self, step):
+        return lax.rem(self.y + (step + NY), NY)
+
+    def zz(self, step):
+        return lax.rem(self.z + (step + NZ), NZ)
+
+    def xx(self, step):
+        return lax.rem(self.x + (step + NX), NX)
+
+    def dev(self, y=0, z=0, flip=False):
+        core = 1 - self.c if flip else self.c
+        return ((self.yy(y) * NZ + self.zz(z)) * 2 + core, self.x)
+
+    def along_x(self, step):
+        return ((self.y * NZ + self.z) * 2 + self.c, self.xx(step))
+
+
+def remote(src, dst, send, recv, device):
+    return pltpu.make_async_remote_copy(
+        src_ref=src, dst_ref=dst, send_sem=send, recv_sem=recv,
+        device_id=device, device_id_type=MESH,
+    )
+
+
+class Gather:
+    def __init__(self, place, w, own, pair, sems):
+        self.p, self.w, self.own, self.pair = place, w, own, pair
+        self.send, self.recv, self.csend, self.crecv, self.psend, self.precv = sems
+
+    def pair_copy(self, part):
+        p = self.p
+        groups = pl.ds(0, 1) if part == 0 else pl.ds(1, GROUPS - 1)
+        return remote(
+            self.own.at[1 - p.c, groups], self.pair.at[groups],
+            self.psend.at[part], self.precv.at[part], p.dev(flip=True),
+        )
+
+    def assemble(self, g):
+        p = self.p
+        mine, theirs = self.own[p.c, g], self.pair[g]
+        first = p.c == 0
+        top = jnp.where(first, mine, theirs)
+        low = jnp.where(first, theirs, mine)
+        columns = pl.ds(pl.multiple_of(p.c * HALF, 128), HALF)
+        self.w[g, p.y, p.z, :, columns] = jnp.concatenate([top, low], axis=0)
+
+    def part(self, g, core, ys, zs):
+        return self.w.at[g, ys, zs, :, core * HALF:(core + 1) * HALF]
+
+    def event(self, core, g, e):
+        p = self.p
+        one = lambda v: pl.ds(v, 1)
+        if core == 0:
+            every = pl.ds(0, NY)
+            if e == 0:
+                return one(p.y), one(p.z), one(p.yy(-1)), one(p.z), 1, 0
+            if e == 1:
+                return one(p.y), one(p.z), one(p.yy(1)), one(p.z), -1, 0
+            if e == 2:
+                d = 1 if g % 2 == 0 else -1
+                return one(p.yy(-d)), one(p.z), one(p.yy(2)), one(p.z), d, 0
+            if e in (9, 10):
+                d = 1 if e == 9 else -1
+                ys = pl.ds(0, 2) if e == 9 else pl.ds(2, 2)
+                return ys, one(p.zz(-3 * d)), ys, one(p.zz(4)), 0, d
+            hop, d = (e - 3) // 2, 1 if (e - 3) % 2 == 0 else -1
+            return every, one(p.zz(-hop * d)), every, one(p.zz(-(hop + 1) * d)), 0, d
+        if e < 6:
+            hop, d = e // 2, 1 if e % 2 == 0 else -1
+            return one(p.y), one(p.zz(-hop * d)), one(p.y), one(p.zz(-(hop + 1) * d)), 0, d
+        if e == 6:
+            d = 1 if g % 2 == 0 else -1
+            return one(p.y), one(p.zz(-3 * d)), one(p.y), one(p.zz(4)), 0, d
+        if e in (7, 8):
+            d = 1 if e == 7 else -1
+            return one(p.y), pl.ds(0, NZ), one(p.yy(-d)), pl.ds(0, NZ), d, 0
+        d = 1 if e == 9 else -1
+        zs = pl.ds(0, NZ // 2) if e == 9 else pl.ds(NZ // 2, NZ // 2)
+        return one(p.yy(-d)), zs, one(p.yy(2)), zs, d, 0
+
+    def copy(self, core, g, e, receive=False):
+        sy, sz, ry, rz, dy, dz = self.event(core, g, e)
+        ref = self.part(g, core, ry, rz) if receive else self.part(g, core, sy, sz)
+        return remote(ref, ref, self.send.at[g, e], self.recv.at[g, e], self.p.dev(dy, dz))
+
+    def chip_copy(self, core, g, e):
+        p = self.p
+        one = lambda v: pl.ds(v, 1)
+        if core == 0:
+            zs = [p.z, p.zz(-1), p.zz(1), p.zz(-2), p.zz(2), p.zz(-3), p.zz(3), p.zz(4)][e]
+            ref = self.part(g, core, pl.ds(0, NY), one(zs))
+        else:
+            ys = [p.y, p.yy(-1), p.yy(1), p.yy(2)][e]
+            ref = self.part(g, core, one(ys), pl.ds(0, NZ))
+        return remote(ref, ref, self.csend.at[g, e], self.crecv.at[g, e], p.dev(flip=True))
+
+    ROUNDS = 7
+
+    def round_of(self, core, g, k):
+        def start(*events):
+            for e in events:
+                self.copy(core, g, e).start()
+
+        def wait(*events):
+            for e in events:
+                self.copy(core, g, e, receive=True).wait_recv()
+
+        def chip(*events):
+            for e in events:
+                self.chip_copy(core, g, e).start()
+
+        if core == 0:
+            if k == 0:
+                start(0, 1)
+            elif k == 1:
+                wait(0, 1); start(2)
+            elif k == 2:
+                wait(2); start(3, 4); chip(0)
+            elif k == 3:
+                wait(3, 4); start(5, 6); chip(1, 2)
+            elif k == 4:
+                wait(5, 6); start(7, 8); chip(3, 4)
+            elif k == 5:
+                wait(7, 8); start(9, 10); chip(5, 6)
+            else:
+                wait(9, 10); chip(7)
+        else:
+            if k == 0:
+                start(0, 1)
+            elif k == 1:
+                wait(0, 1); start(2, 3)
+            elif k == 2:
+                wait(2, 3); start(4, 5)
+            elif k == 3:
+                wait(4, 5); start(6)
+            elif k == 4:
+                wait(6); start(7, 8); chip(0)
+            elif k == 5:
+                wait(7, 8); start(9, 10); chip(1, 2)
+            else:
+                wait(9, 10); chip(3)
+
+    def tick(self, rounds):
+        for core in (0, 1):
+            @pl.when(self.p.c == core)
+            def _():
+                for g, k in rounds:
+                    self.round_of(core, g, k)
+
+    def finish(self, g):
+        for core in (0, 1):
+            @pl.when(self.p.c == core)
+            def _():
+                for e in range(4 if core == 0 else 8):
+                    self.chip_copy(1 - core, g, e).wait_recv()
+
+    def drain(self):
+        for core in (0, 1):
+            @pl.when(self.p.c == core)
+            def _():
+                for g in range(GROUPS):
+                    for e in range(EVENTS):
+                        self.copy(core, g, e).wait_send()
+                    for e in range(8 if core == 0 else 4):
+                        self.chip_copy(core, g, e).wait_send()
+        for part in (0, 1):
+            self.pair_copy(part).wait_send()
+
+
+GATHER_SEMS = [
+    pltpu.SemaphoreType.DMA((GROUPS, EVENTS)), pltpu.SemaphoreType.DMA((GROUPS, EVENTS)),
+    pltpu.SemaphoreType.DMA((GROUPS, CHIP_EVENTS)), pltpu.SemaphoreType.DMA((GROUPS, CHIP_EVENTS)),
+    pltpu.SemaphoreType.DMA((2,)), pltpu.SemaphoreType.DMA((2,)),
+]
+
+
+def greet(devices):
+    barrier = pltpu.get_barrier_semaphore()
+    for device in devices:
+        pl.semaphore_signal(barrier, inc=1, device_id=device, device_id_type=MESH)
+    pl.semaphore_wait(barrier, len(devices))
+
+
+class Reduce:
+    def __init__(self, place, parts, relay, got, send, recv):
+        self.p, self.parts, self.relay, self.got = place, parts, relay, got
+        self.s, self.r = send, recv
+        self.d = 1 - 2 * place.c
+
+    def copies(self):
+        p, d = self.p, self.d
+        a = remote(self.parts.at[p.xx(2)], self.relay, self.s.at[0], self.r.at[0], p.along_x(d))
+        b = remote(self.parts.at[p.xx(1)], self.got.at[0], self.s.at[1], self.r.at[1], p.along_x(1))
+        c = remote(self.parts.at[p.xx(-1)], self.got.at[1], self.s.at[2], self.r.at[2], p.along_x(-1))
+        e = remote(self.relay, self.got.at[2], self.s.at[3], self.r.at[3], p.along_x(d))
+        return a, b, c, e
+
+    def begin(self):
+        a, b, c, _ = self.copies()
+        a.start(); b.start(); c.start()
+
+    def middle(self):
+        a, _, _, e = self.copies()
+        a.wait_recv(); e.start()
+
+    def end(self):
+        _, b, c, e = self.copies()
+        b.wait_recv(); c.wait_recv(); e.wait_recv()
+
+    def drain(self):
+        for copy in self.copies():
+            copy.wait_send()
+
+    def total(self):
+        f = jnp.float32
+        return ((self.parts[self.p.x].astype(f) + self.got[0].astype(f))
+                + (self.got[1].astype(f) + self.got[2].astype(f)))
+
+
+class Spread:
+    def __init__(self, place, full, send, recv):
+        self.p, self.full, self.s, self.r = place, full, send, recv
+        self.d = 1 - 2 * place.c
+
+    def copies(self, receive=False):
+        p, d = self.p, self.d
+        at = self.full.at
+        return (
+            remote(at[p.xx(-1) if receive else p.x], at[p.xx(-1) if receive else p.x], self.s.at[0], self.r.at[0], p.along_x(1)),
+            remote(at[p.xx(1) if receive else p.x], at[p.xx(1) if receive else p.x], self.s.at[1], self.r.at[1], p.along_x(-1)),
+            remote(at[p.xx(2) if receive else p.xx(-d)], at[p.xx(2) if receive else p.xx(-d)], self.s.at[2], self.r.at[2], p.along_x(d)),
+        )
+
+    def begin(self):
+        a, b, _ = self.copies()
+        a.start(); b.start()
+
+    def middle(self):
+        a, b, _ = self.copies(receive=True)
+        a.wait_recv(); b.wait_recv()
+        self.copies()[2].start()
+
+    def end(self):
+        self.copies(receive=True)[2].wait_recv()
+
+    def drain(self):
+        for copy in self.copies():
+            copy.wait_send()
+
+
+def gather_kernel(own, out, w, pair, sem, *sems):
+    p = Place()
+    greet([p.dev(flip=True), p.dev(y=1), p.dev(y=-1), p.dev(z=1), p.dev(z=-1)])
+    gather = Gather(p, w, own, pair, sems)
+    gather.pair_copy(0).start()
+    gather.pair_copy(1).start()
+    gather.pair_copy(0).wait_recv()
+    gather.assemble(0)
+    gather.tick([(0, 0)])
+    gather.pair_copy(1).wait_recv()
+    for g in range(1, GROUPS):
+        gather.assemble(g)
+    stride = 1
+    for t in range(1, stride * (GROUPS - 1) + 7):
+        gather.tick([(g, t - stride * g) for g in range(GROUPS) if 0 <= t - stride * g < 7])
+    for g in range(GROUPS):
+        gather.finish(g)
+        pltpu.make_async_copy(w.at[g], out.at[g], sem.at[g]).start()
+    gather.drain()
+    for g in range(GROUPS):
+        pltpu.make_async_copy(w.at[g], out.at[g], sem.at[g]).wait()
+
+
+def gather_weights(own):
+    return pl.pallas_call(
+        gather_kernel,
+        out_shape=jax.ShapeDtypeStruct((GROUPS, NY, NZ, 2 * SHARD, D), jnp.bfloat16),
+        in_specs=[pl.BlockSpec(memory_space=pltpu.VMEM)],
+        out_specs=pl.BlockSpec(memory_space=pl.ANY),
+        scratch_shapes=[
+            pltpu.VMEM((GROUPS, NY, NZ, 2 * SHARD, D), jnp.bfloat16),
+            pltpu.VMEM((GROUPS, SHARD, HALF), jnp.bfloat16),
+            pltpu.SemaphoreType.DMA((GROUPS,)),
+        ] + GATHER_SEMS,
+        compiler_params=pltpu.CompilerParams(
+            collective_id=0, has_side_effects=True, vmem_limit_bytes=50 << 20
+        ),
+        name="gather_weights",
+    )(own)
+
 
 HEAD_DIM = 80
 GRID = 16
 
 
 EPS = 1e-06
-
-
-def for_sending(shard):
-
-    def short(part):
-        return part.astype(jnp.bfloat16) if part.dtype == jnp.float32 else part
-
-    return jax.tree.map(short, shard)
 
 
 def normalize(stream):
@@ -23,14 +328,6 @@
     center = values_f - jnp.mean(values_f, axis=-1, keepdims=True)
     spread = jnp.mean(center * center, axis=-1, keepdims=True)
     return (center * lax.rsqrt(spread + EPS)).astype(jnp.bfloat16)
-
-
-def fetch_weights(weights):
-    return jax.tree.map(
-        lambda part, own: part.astype(own.dtype),
-        lax.all_gather(for_sending(weights), "req", axis=0, tiled=True),
-        weights,
-    )
 
 
 def tensor_total(partial_value):
@@ -106,11 +403,15 @@
     key_valid = ((patch_index // GRID)[None, :] < 2 * half_grid[:, 0:1]) & (
         (patch_index % GRID)[None, :] < 2 * half_grid[:, 1:2]
     )
-    enc_weights = fetch_weights((enc_qkv, enc_out_t, enc_up, enc_down_t))
+    own = jnp.concatenate(
+        [enc_qkv, enc_out_t, enc_up, enc_down_t, merge_t, dec_qkv, dec_out_t, dec_up, dec_down_t], axis=1
+    )
+    own = own.reshape(SHARD, GROUPS, 2, HALF).transpose(2, 1, 0, 3)
+    w = gather_weights(own).reshape(GROUPS, D, D)
+    enc_weights = (w[0, :, :960], w[0, :, 960:], w[1], w[2])
+    merge_local = w[3]
+    qkv_dec, out_dec, up_dec, down_dec = w[4, :, :960], w[4, :, 960:], w[5], w[6]
     encoded = transformer_layer(patches, enc_weights, key_valid[:, None, None, :], image_count)
-    merge_local, qkv_dec, out_dec, up_dec, down_dec = fetch_weights(
-        (merge_t, dec_qkv, dec_out_t, dec_up, dec_down_t)
-    )
     half_side = GRID // 2
     blocks = encoded.reshape(image_count, half_side, 2, half_side, 2, model_width).transpose(
         0, 1, 3, 2, 4, 5

time: 854 us -> 441 us (0.52)
  waiting for transfers between devices: 598 us -> 221 us
  blocking collectives: 108 us -> 0 us
  Pallas kernels: 0 us -> 98.8 us
  local copies, waits for them, and re-layouts: 69.4 us -> 39.3 us
    all_gather x7 -> x0, waiting for transfers between devices: 384 us -> none  [fetch_weights(): lax.all_gather(for_sending(weights), 'req', axis=0, tiled=True)]
    all_gather x2 -> x0, blocking collectives: 108 us -> none  [fetch_weights(): lax.all_gather(for_sending(weights), 'req', axis=0, tiled=True)]
    pallas_call x0 -> x1, Pallas kernels: none -> 98.8 us  [gather_weights(): pl.pallas_call(gather_kernel, out_shape=jax.ShapeDtypeStruct((GROUPS, NY,...]
    unnamed x21 -> x12, local copies, waits for them, and re-layouts: 42.5 us -> 0.99 us
    all_to_all x1, waiting for transfers between devices: 0.01 us -> 11.5 us  [on_device(): lax.all_to_all(outgoing, 'req', split_axis=0, concat_axis=0, tiled=True)]
    slice x0 -> x1, local copies, waits for them, and re-layouts: none -> 10.9 us  [on_device(): enc_weights = (w[0, :, :960], w[0, :, 960:], w[1], w[2])]
  transfers between devices with their start and end apart: 14 -> 7, of which waited for: 12 -> 6; matrix products, arithmetic and copies ran while one was open for 8% -> 7% of each run, Pallas kernels for 0% -> 0%
where the time goes in v1:
time: 441 us; the launch traced here: 440 us
  waiting for transfers between devices  221 us (50%)
  Pallas kernels  98.8 us (22%)
  local copies, waits for them, and re-layouts  39.3 us (9%)
  matrix products  32 us (7%)
  starting transfers between devices  21.8 us (5%)
  between operations  15.4 us (3%)
  other arithmetic  10.9 us (2%)
    psum x5, waiting for transfers between devices, tensor_total(): lax.psum(partial_value.astype(jnp.bfloat16), 'tp').astype(jnp.float32)  210 us
    pallas_call x1, Pallas kernels, gather_weights(): pl.pallas_call(gather_kernel, out_shape=jax.ShapeDtypeStruct((GROUPS, NY,...  98.8 us
    dot_general x2, matrix products, feed_forward(): lax.dot_general(hidden, w_down_t, (((1,), (1,)), ((), ())), preferred_ele...  15.8 us
    all_to_all x1, waiting for transfers between devices, on_device(): lax.all_to_all(outgoing, 'req', split_axis=0, concat_axis=0, tiled=True)  11.5 us
    slice x1, local copies, waits for them, and re-layouts, on_device(): enc_weights = (w[0, :, :960], w[0, :, 960:], w[1], w[2])  10.9 us
    all_to_all x1, starting transfers between devices, on_device(): lax.all_to_all(outgoing, 'req', split_axis=0, concat_axis=0, tiled=True)  10.9 us
    all_to_all x1, starting transfers between devices, on_device(): lax.all_to_all(out_pos, 'req', split_axis=0, concat_axis=0, tiled=True)  10.6 us
    scatter x1, local copies, waits for them, and re-layouts, on_device(): outgoing = jnp.zeros((senders, capacity, model_width), jnp.bfloat16).at[d...  9.99 us
  transfers between devices with their start and end apart: 7, of which 6 were waited for; matrix products, arithmetic and copies ran while one was open for 7% of the time, Pallas kernels for 0%

profile of v1, /device:TPU:8, one launch (start us, length us, event | category | flops | bytes accessed | tf_op | source)
XLA Modules:
  0.0 439.7 jit_solution(1388381963629248762)
XLA Ops:
  6.5 1.1 concatenate.8
  7.7 0.1 reshape.259
  7.9 98.8 %gather_weights.1 = bf16[7,4,8,40,1280]{4,3,2,1,0:T(8,128)(2,1)} custom-call(bf16[2,7,20,640]{3,2,1,0:T(8,128)(2,1)S(1)} %bitcast.115), custom_call_target="tpu_custom_call" | custom-call | tf_op jit(solution)/shard_map/gather_weights/pallas_call | solution.py:302
  106.7 0.2 convert_reduce_fusion.1
  106.9 0.3 fusion.14
  107.2 0.1 copy-done.4
  107.3 0.6 fusion.219
  109.3 2.9 fusion.30
  112.3 0.3 fusion.11
  112.6 0.5 fusion.220
  113.1 0.4 convolution_convert_fusion.6
  113.5 2.9 convolution_convert_fusion
  116.4 0.0 all-reduce.6.cloned.1.call-update
  116.4 0.2 all-reduce.8.cloned.1.call-start
  116.6 10.9 %fusion.218 = (bf16[1,4,8,40,1280]{4,3,2,1,0:T(8,128)(2,1)}, bf16[1,4,8,40,1280]{4,3,2,1,0:T(8,128)(2,1)}, bf16[1,4,8,40,1280]{4,3,2,1,0:T(8,128)(2,1)}, bf16[1,...) fusion(bf16[7,4,8,40,1280]{4,3,2,1,0:T(8,128)(2,1)} %gather_weights.1), kind=kLoop, calls=%fused_computation.285 | loop fusion | bytes 32768000 | tf_op jit(solution)/shard_map/slice | solution.py:411
  127.6 36.9 %all-reduce.6.cloned.1.call-done = bf16[256,1280]{1,0:T(8,128)(2,1)} async-done(((bf16[256,1280]{1,0:T(8,128)(2,1)}), bf16[256,1280]{1,0:T(8,128)(2,1)}) %all-reduce.6.cloned.1.call-update) | async-done | bytes 655376 | tf_op jit(solution)/shard_map/psum | solution.py:334
  164.5 1.6 convert_reduce_fusion
  166.1 0.8 copy-done.2
  166.9 0.3 fusion.12
  167.2 8.4 %convolution_convert_fusion.1 = bf16[256,1280]{1,0:T(8,128)(2,1)} fusion(bf16[1280,1280]{1,0:T(8,128)(2,1)} %bitcast.125, bf16[1280,1280]{1,0:T(8,128)(2,1)} %bitcast.124, bf16[256,1280]{1,0:T(8,128)(2,1)} %copy-done.2, f32[256]{0:T(256)S(1)} %add_rsqrt_fusion.2, f32[256]{0:T(256)S(1)} %broadcast_multiply_fusion.2), kind=kOutput, calls=%fused_computation.10 | convolution fusion | flops 1700659200 | bytes 7866368 | tf_op jit(solution)/shard_map/dot_general | solution.py:366
  175.7 0.0 all-reduce.8.cloned.1.call-update
  175.7 0.0 all-reduce.10.cloned.1.call-start
  175.7 0.1 fusion.142
  175.8 0.1 reduce_window_sum.11
  175.9 0.2 select_reduce_fusion
  176.1 49.3 %all-reduce.8.cloned.1.call-done = bf16[256,1280]{1,0:T(8,128)(2,1)} async-done(((bf16[256,1280]{1,0:T(8,128)(2,1)}), bf16[256,1280]{1,0:T(8,128)(2,1)}) %all-reduce.8.cloned.1.call-update) | async-done | bytes 655376 | tf_op jit(solution)/shard_map/psum | solution.py:334
  225.4 2.3 fusion.17
  227.7 2.6 reshape.266
  230.3 2.4 copy.59
  232.7 2.9 reshape.267
  235.6 2.7 convolution_convert_fusion.4
  238.3 0.0 all-reduce.10.cloned.1.call-update
  238.4 1.3 and_select_fusion.2
  239.7 3.5 scatter_fusion
  243.2 0.7 copy.37
  243.9 10.6 %all-to-all-start = ((s32[64,1,2]{2,1,0:T(1,128)}), s32[64,1,2]{2,1,0:T(1,128)S(1)}, u32[]{:S(2)}, u32[]{:S(2)}) async-start(s32[64,1,2]{2,1,0:T(1,128)} %copy.37), calls=%async_computation | async-start | bytes 65536 | tf_op jit(solution)/shard_map/all_to_all | solution.py:452
  254.5 31.3 %all-reduce.10.cloned.1.call-done = bf16[64,1280]{1,0:T(8,128)(2,1)} async-done(((bf16[64,1280]{1,0:T(8,128)(2,1)}), bf16[64,1280]{1,0:T(8,128)(2,1)}) %all-reduce.10.cloned.1.call-update) | async-done | bytes 163856 | tf_op jit(solution)/shard_map/psum | solution.py:334
  285.7 0.9 broadcast_in_dim.47
  286.6 10.0 %scatter_fusion.1 = bf16[64,2,1280]{2,1,0:T(2,128)(2,1)} fusion(bf16[64,2,1280]{2,1,0:T(2,128)(2,1)} %broadcast_in_dim.47, s32[64]{0:T(128)S(1)} %fusion.150, bf16[64,1280]{1,0:T(8,128)(2,1)} %all-reduce.10.cloned.1.call-done), kind=kCustom, calls=%fused_computation.1 | custom fusion | bytes 492032 | tf_op jit(solution)/shard_map/scatter | solution.py:443
  296.6 10.9 %all-to-all-start.1 = ((bf16[64,2,1280]{2,1,0:T(2,128)(2,1)}), bf16[64,2,1280]{2,1,0:T(2,128)(2,1)S(1)}, u32[]{:S(2)}, u32[]{:S(2)}) async-start(bf16[64,2,1280]{2,1,0:T(2,128)(2,1)} %scatter_fusion.1), calls=%async_computation.1 | async-start | bytes 655360 | tf_op jit(solution)/shard_map/all_to_all | solution.py:451
  307.5 0.0 all-reduce.12.cloned.1.call-start
  307.6 0.5 broadcast.367
  308.1 0.6 reduce.11
  308.7 0.1 all_to_all.13
  308.9 11.5 %all-to-all-done.1 = bf16[64,2,1280]{2,1,0:T(2,128)(2,1)S(1)} async-done(((bf16[64,2,1280]{2,1,0:T(2,128)(2,1)}), bf16[64,2,1280]{2,1,0:T(2,128)(2,1)S(1)}, u32[]{:S(2)}, u32[]{:S(2)}) %all-to-all-start.1) | async-done | bytes 327712 | tf_op jit(solution)/shard_map/all_to_all | solution.py:451
  320.4 0.1 reshape.290
  320.5 1.4 scatter_fusion.2
  322.0 0.1 convert_reduce_fusion.3
  322.1 0.3 fusion.38
  322.4 2.5 fusion.31
  324.9 0.2 copy.44
  325.1 0.3 fusion.29
  325.4 0.5 fusion.221
  325.9 0.3 convolution_convert_fusion.5
  326.2 2.8 convolution_convert_fusion.3
  329.0 0.0 all-reduce.12.cloned.1.call-update
  329.0 0.0 all-reduce.14.cloned.1.call-start
  329.0 44.5 %all-reduce.12.cloned.1.call-done = bf16[192,1280]{1,0:T(8,128)(2,1)} async-done(((bf16[192,1280]{1,0:T(8,128)(2,1)}), bf16[192,1280]{1,0:T(8,128)(2,1)}) %all-reduce.12.cloned.1.call-update) | async-done | bytes 491536 | tf_op jit(solution)/shard_map/psum | solution.py:334
  373.5 1.3 convert_reduce_fusion.2
  374.8 0.3 fusion.36
  375.1 7.4 %convolution_convert_fusion.2 = bf16[192,1280]{1,0:T(8,128)(2,1)} fusion(bf16[1280,1280]{1,0:T(8,128)(2,1)} %bitcast.122, bf16[1280,1280]{1,0:T(8,128)(2,1)} %bitcast.123, bf16[192,1280]{1,0:T(8,128)(2,1)S(1)} %get-tuple-element.6, f32[192]{0:T(256)S(1)} %add_rsqrt_fusion, f32[192]{0:T(256)S(1)} %broadcast_multiply_fusion), kind=kOutput, calls=%fused_computation.11 | convolution fusion | flops 1275494400 | bytes 7538176 | tf_op jit(solution)/shard_map/dot_general | solution.py:366
  382.5 0.0 all-reduce.14.cloned.1.call-update
  383.1 48.0 %all-reduce.14.cloned.1.call-done = bf16[192,1280]{1,0:T(8,128)(2,1)} async-done(((bf16[192,1280]{1,0:T(8,128)(2,1)}), bf16[192,1280]{1,0:T(8,128)(2,1)}) %all-reduce.14.cloned.1.call-update) | async-done | bytes 491536 | tf_op jit(solution)/shard_map/psum | solution.py:334
  431.2 2.0 fusion.97
  (27 shorter events, 0.2 us)
Async XLA Ops:
  6.5 157.9 %all-reduce.6.cloned.1.call-start = ((), (), s32[]{:S(2)}) async-start(), calls=%async_computation.2 | async-start | bytes 1310720 | tf_op jit(solution)/shard_map/psum | solution.py:334
  7.8 98.8 %copy-start.1 = (bf16[256,1280]{1,0:T(8,128)(2,1)S(1)}, bf16[256,1280]{1,0:T(8,128)(2,1)}, u32[]{:S(2)}) copy-start(bf16[256,1280]{1,0:T(8,128)(2,1)} %param.15) | copy-start | bytes 1966084
  106.7 0.7 copy-start.4
  116.4 109.0 %all-reduce.8.cloned.1.call-start = ((), (), s32[]{:S(2)}) async-start(), calls=%async_computation.3 | async-start | bytes 1310720 | tf_op jit(solution)/shard_map/psum | solution.py:334
  166.0 0.8 copy-start.2
  167.2 8.5 %copy-start.3 = (s32[64]{0:T(128)S(1)}, s32[64]{0:T(128)}, u32[]{:S(2)}) copy-start(s32[64]{0:T(128)} %param.18) | copy-start | bytes 772
  175.7 110.0 %all-reduce.10.cloned.1.call-start = ((), (), s32[]{:S(2)}) async-start(), calls=%async_computation.4 | async-start | bytes 327680 | tf_op jit(solution)/shard_map/psum | solution.py:334
  235.6 2.8 copy-start.5
  243.9 52.7 %all-to-all-start = ((s32[64,1,2]{2,1,0:T(1,128)}), s32[64,1,2]{2,1,0:T(1,128)S(1)}, u32[]{:S(2)}, u32[]{:S(2)}) async-start(s32[64,1,2]{2,1,0:T(1,128)} %copy.37), calls=%async_computation | async-start | bytes 65536 | tf_op jit(solution)/shard_map/all_to_all | solution.py:452
  296.6 23.9 %copy-start = (bf16[192,1280]{1,0:T(8,128)(2,1)S(1)}, bf16[192,1280]{1,0:T(8,128)(2,1)}, u32[]{:S(2)}) copy-start(bf16[192,1280]{1,0:T(8,128)(2,1)} %param.17) | copy-start | bytes 1474564
  296.6 23.8 %all-to-all-start.1 = ((bf16[64,2,1280]{2,1,0:T(2,128)(2,1)}), bf16[64,2,1280]{2,1,0:T(2,128)(2,1)S(1)}, u32[]{:S(2)}, u32[]{:S(2)}) async-start(bf16[64,2,1280]{2,1,0:T(2,128)(2,1)} %scatter_fusion.1), calls=%async_computation.1 | async-start | bytes 655360 | tf_op jit(solution)/shard_map/all_to_all | solution.py:451
  307.5 66.0 %all-reduce.12.cloned.1.call-start = ((), (), s32[]{:S(2)}) async-start(), calls=%async_computation.5 | async-start | bytes 983040 | tf_op jit(solution)/shard_map/psum | solution.py:334
  329.0 102.2 %all-reduce.14.cloned.1.call-start = ((), (), s32[]{:S(2)}) async-start(), calls=%async_computation.6 | async-start | bytes 983040 | tf_op jit(solution)/shard_map/psum | solution.py:334
Sparse Core Ops, SparseCore 0:
  116.5 47.9 all-reduce.5
  175.8 49.5 all-reduce.7
  238.5 47.2 all-reduce.9
  329.1 44.3 all-reduce.11
  382.6 48.4 all-reduce.13
